TPU v7x, 32 devices: a whole 2x2x4 slice. The times are simulated.
32 devices in a mesh: tm: 8 (over y, x, core), grp: 4 (over z).
Axes of the slice: x: 2, y: 2, z: 4, core: 2. Of those that a mesh axis runs over, the one named last changes fastest.
Arguments:
- series: float32 [131072, 512], P(('tm', 'grp')), may hold values from -6 to 6
- filter_taps: float32 [33], replicated, may hold values from -1 to 1
- sign_flips: int32 [131072], P(('tm', 'grp')), may hold values from -1 to 1, as said below
- samples: int32 [8192], replicated, may hold values from 0 to 131071, as said below
Outputs:
- sketch: float32 [8192, 512], P(('tm', 'grp'))
- r_factor: float32 [512, 512], replicated
Inputs may be any that keep to these rules, and one draw needn't show every extreme that they name: `sign_flips`: each entry is -1 or +1. All distinct; the values of samples modulo 4096 take exactly 4096 distinct values, each by exactly 2 consecutive entries; entries are ordered by their value modulo 4096, then by value.
All inputs are finite; a program needn't handle non-finite values.
Results may differ from a plain program's by a relative error of at most 0.0003.
Values sent between devices are 32-bit elements; how exact they have to be, the bound alone decides.
A program may use at most 128 MiB of HBM per device.

v0:
```python
import jax
import jax.numpy as jnp
from jax import lax
from jax.sharding import PartitionSpec as P


def extended(block, sides, width):
    for axis, dim in sides:
        count = lax.axis_size(axis)
        forward = [(i, i + 1) for i in range(count - 1)]
        backward = [(target, source) for source, target in forward]
        low = lax.ppermute(
            lax.slice_in_dim(block, block.shape[dim] - width, None, axis=dim), axis, forward
        )
        high = lax.ppermute(lax.slice_in_dim(block, 0, width, axis=dim), axis, backward)
        block = jnp.concatenate([low, block, high], axis=dim)
    return block


def bit_count(values, width_bits):
    counted = jnp.zeros_like(values)
    for offset in range(width_bits):
        counted = counted + (values >> offset & 1)
    return counted


def hadamard(order):
    row_ids = jnp.arange(order, dtype=jnp.int32)[:, None]
    col_ids = jnp.arange(order, dtype=jnp.int32)[None, :]
    parity = bit_count(row_ids & col_ids, max(order.bit_length(), 1)) & 1
    return (1 - 2 * parity).astype(jnp.float32)


def local_transform(rows_block):
    length, columns = rows_block.shape
    levels = length.bit_length() - 1
    outer = 2 ** ((levels + 1) // 2)
    inner = length // outer
    layered = rows_block.reshape(outer, inner, columns)
    layered = jnp.einsum("ux,xvw->uvw", hadamard(outer), layered, precision=lax.Precision.HIGHEST)
    layered = jnp.einsum("vy,uyw->uvw", hadamard(inner), layered, precision=lax.Precision.HIGHEST)
    return layered.reshape(length, columns)


def on_device(series, filter_taps, sign_flips, samples):
    rows_dev = series.shape[0]
    columns = series.shape[1]
    tap_count = filter_taps.shape[0]
    half_taps = (tap_count - 1) // 2
    devices_all = lax.axis_size("tm") * lax.axis_size("grp")
    total_rows = rows_dev * devices_all
    sample_count = samples.shape[0]
    padded = extended(series, ((("tm", "grp"), 0),), half_taps)
    filtered = filter_taps[0] * padded[0:rows_dev]
    for offset in range(1, tap_count):
        filtered = filtered + filter_taps[offset] * padded[offset : offset + rows_dev]
    flipped = filtered * sign_flips.astype(jnp.float32)[:, None]
    mixed = local_transform(flipped)
    position = lax.axis_index("tm") * lax.axis_size("grp") + lax.axis_index("grp")
    row_scale = 1.0 / jnp.sqrt(jnp.float32(total_rows))
    block_rows = sample_count // devices_all
    copies = max(2, sample_count // rows_dev)
    distinct = sample_count // copies
    per_device = distinct // devices_all
    used_positions = samples[::copies] % rows_dev
    outgoing = jnp.take(mixed, used_positions, axis=0)
    incoming = lax.all_to_all(outgoing, ("tm", "grp"), split_axis=0, concat_axis=0, tiled=True)
    stacked = incoming.reshape(devices_all, per_device, columns)
    combined = (
        jnp.einsum("op,pkw->okw", hadamard(devices_all), stacked, precision=lax.Precision.HIGHEST)
        * row_scale
    )
    combined = combined.reshape(devices_all * per_device, columns)
    mine = lax.dynamic_slice_in_dim(samples, position * block_rows, block_rows)
    slot_index = mine // rows_dev * per_device + jnp.arange(block_rows, dtype=jnp.int32) // copies
    sketch = jnp.take(combined, slot_index, axis=0)
    local_gram = lax.dot_general(
        sketch,
        sketch,
        (((0,), (0,)), ((), ())),
        precision=lax.Precision.HIGHEST,
        preferred_element_type=jnp.float32,
    )
    gram = lax.psum(local_gram, ("tm", "grp"))
    lower = jnp.linalg.cholesky(gram / sample_count)
    return (sketch, lower.T)


def solution(mesh):
    return jax.shard_map(
        on_device,
        mesh=mesh,
        in_specs=(P(("tm", "grp"), None), P(), P(("tm", "grp")), P()),
        out_specs=(P(("tm", "grp"), None), P()),
        check_vma=False,
    )
```

profile of v0, /device:TPU:0, one launch (start us, length us, event | category | flops | bytes accessed | tf_op | source)
XLA Modules:
  0.0 659.5 jit_solution(13701622514079241855)
XLA Ops:
  7.2 0.8 fusion.110
  7.9 4.9 collective-permute-start
  12.9 1.3 collective-permute-start.1
  14.2 1.4 slice.317
  15.6 2.1 fusion.111
  17.7 1.9 fusion.112
  19.6 0.7 convert_element_type.14
  20.3 0.0 collective-permute-done
  20.3 0.6 constant_dynamic-update-slice_fusion.1
  20.9 11.5 %constant_dynamic-update-slice_fusion = (f32[4112,512]{1,0:T(8,128)}, f32[4112,512]{1,0:T(8,128)}) fusion(f32[4112,512]{1,0:T(8,128)} %constant_dynamic-update-slice_fusion.1, f32[4096,512]{1,0:T(8,128)} %param.4), kind=kLoop, calls=%fused_computation.143 | loop fusion | bytes 25165824 | tf_op jit(solution)/shard_map/concatenate | solution.py:16
  32.4 0.0 collective-permute-done.1
  32.4 0.6 constant_dynamic-update-slice_fusion.2
  33.0 122.8 %fusion.1 = f32[4096,512]{1,0:T(8,128)S(1)} fusion(f32[4112,512]{1,0:T(8,128)} %constant_dynamic-update-slice_fusion.2, f32[4112,512]{1,0:T(8,128)} %get-tuple-element.10, f32[4096,512]{1,0:T(8,128)} %param.4, f32[4096]{0:T(1024)S(1)} %convert_element_type.14, f32[]{:T(128)} %bitcast.35, f32[]{:T(128)} %bitcast.34, f32[]{:T(128)} %bitcast.33, f32[]{:T(128)} %bitcast.32, ...), kind=kLoop, calls=%fused_computation.4 | loop fusion | flops 138412032 | bytes 285229184 | tf_op jit(solution)/shard_map/mul | solution.py:57
  155.8 12.4 %fusion.37 = f32[64,64,512]{2,0,1:T(8,128)S(1)} fusion(f32[64,64,512]{2,1,0:T(8,128)S(1)} %bitcast.77), kind=kOutput, calls=%fused_computation.71 | convolution fusion | flops 1610715136 | bytes 16777216 | tf_op jit(solution)/shard_map/ux,xvw->uvw/dot_general | solution.py:40
  168.3 13.8 %fusion.35 = f32[64,512,64]{1,2,0:T(8,128)} fusion(f32[64,64,512]{2,0,1:T(8,128)S(1)} %fusion.37), kind=kOutput, calls=%fused_computation.69 | convolution fusion | flops 1610715136 | bytes 16777216 | tf_op jit(solution)/shard_map/vy,uyw->uvw/dot_general | solution.py:41
  182.1 21.4 %gather_fusion = f32[4096,512]{1,0:T(8,128)} fusion(f32[4096,512]{1,0:T(8,128)} %bitcast.75, s32[4096]{0:T(1024)S(1)} %broadcast_clamp_fusion), kind=kCustom, calls=%fused_computation | custom fusion | bytes 16793600 | tf_op jit(solution)/shard_map/jit(_take)/gather | solution.py:66
  203.5 5.8 broadcast_select_fusion
  209.3 7.0 %all-to-all-start = ((f32[32,128,512]{2,1,0:T(8,128)}), f32[32,128,512]{2,1,0:T(8,128)}, u32[]{:S(2)}, u32[]{:S(2)}) async-start(f32[32,128,512]{2,1,0:T(8,128)} %broadcast_select_fusion), calls=%async_computation | async-start | bytes 16777216 | tf_op jit(solution)/shard_map/all_to_all | solution.py:67
  216.3 0.0 all-reduce.3.cloned.1.call-start
  216.4 0.8 compare_and_fusion
  217.2 180.5 %all-to-all-done = f32[32,128,512]{2,1,0:T(8,128)} async-done(((f32[32,128,512]{2,1,0:T(8,128)}), f32[32,128,512]{2,1,0:T(8,128)}, u32[]{:S(2)}, u32[]{:S(2)}) %all-to-all-start) | async-done | bytes 8388640 | tf_op jit(solution)/shard_map/all_to_all | solution.py:67
  397.7 16.9 %broadcast_multiply_fusion = f32[32,128,512]{2,0,1:T(8,128)S(1)} fusion(f32[32,128,512]{2,1,0:T(8,128)} %all-to-all-done), kind=kOutput, calls=%fused_computation.73 | convolution fusion | flops 807426048 | bytes 16777216 | tf_op jit(solution)/shard_map/op,pkw->okw/dot_general | solution.py:70
  414.6 8.1 %copy.18 = f32[32,128,512]{2,1,0:T(8,128)} copy(f32[32,128,512]{2,0,1:T(8,128)S(1)} %broadcast_multiply_fusion) | data formatting | bytes 16777216 | tf_op jit(solution)/shard_map/mul | solution.py:70
  422.7 4.6 gather_fusion.1
  427.3 0.1 broadcast_select_fusion.1
  427.4 0.0 copy-start
  427.4 2.0 fusion.113
  429.4 0.0 all-reduce.3.cloned.1.call-update
  429.4 134.7 %all-reduce.3.cloned.1.call-done = f32[512,512]{0,1:T(8,128)} async-done(((f32[512,512]{0,1:T(8,128)}), f32[512,512]{0,1:T(8,128)}) %all-reduce.3.cloned.1.call-update) | async-done | bytes 1048592 | tf_op jit(solution)/shard_map/psum | solution.py:84
  564.1 1.3 broadcast_multiply_fusion.1
  565.5 0.3 copy.20
  565.8 1.5 fusion.41
  567.3 11.7 %cholesky.104 = f32[128,128]{1,0:T(8,128)S(1)} custom-call(f32[128,128]{1,0:T(8,128)S(1)} %cholesky.266), custom_call_target="Cholesky" | custom-call | tf_op jit(solution)/shard_map/jit(cholesky)/cholesky | solution.py:85
  579.0 0.1 cholesky.224
  579.2 10.0 %custom-call.27 = f32[1,128,128]{1,2,0:T(8,128)S(1)} custom-call(f32[1,128,128]{2,1,0:T(8,128)S(1)} %get-tuple-element.23), custom_call_target="InvertDiagBlocksLowerTriangular" | custom-call | tf_op jit(solution)/shard_map/jit(cholesky)/cholesky | solution.py:85
  589.2 0.3 constant_dynamic-update-slice_fusion.6
  589.5 0.3 convolution_subtract_fusion
  589.8 11.7 %cholesky.217 = f32[128,128]{1,0:T(8,128)S(1)} custom-call(f32[128,128]{1,0:T(8,128)S(1)} %cholesky.270), custom_call_target="Cholesky" | custom-call | tf_op jit(solution)/shard_map/jit(cholesky)/cholesky | solution.py:85
  601.6 9.8 %custom-call.28 = f32[1,128,128]{1,2,0:T(8,128)S(1)} custom-call(f32[1,128,128]{2,1,0:T(8,128)S(1)} %get-tuple-element.20), custom_call_target="InvertDiagBlocksLowerTriangular" | custom-call | tf_op jit(solution)/shard_map/jit(cholesky)/cholesky | solution.py:85
  611.4 0.3 convolution_dynamic-update-slice_fusion
  611.7 0.4 convolution_subtract_fusion.1
  612.1 11.9 %cholesky.238 = f32[128,128]{1,0:T(8,128)S(1)} custom-call(f32[128,128]{1,0:T(8,128)S(1)} %cholesky.275), custom_call_target="Cholesky" | custom-call | tf_op jit(solution)/shard_map/jit(cholesky)/cholesky | solution.py:85
  624.0 9.8 %custom-call.29 = f32[1,128,128]{1,2,0:T(8,128)S(1)} custom-call(f32[1,128,128]{2,1,0:T(8,128)S(1)} %get-tuple-element.17), custom_call_target="InvertDiagBlocksLowerTriangular" | custom-call | tf_op jit(solution)/shard_map/jit(cholesky)/cholesky | solution.py:85
  633.9 0.2 convolution_dynamic-update-slice_fusion.1
  634.1 0.4 convolution_subtract_fusion.2
  634.5 11.7 %cholesky.255 = f32[128,128]{1,0:T(8,128)S(1)} custom-call(f32[128,128]{1,0:T(8,128)S(1)} %convolution_subtract_fusion.2), custom_call_target="Cholesky" | custom-call | tf_op jit(solution)/shard_map/jit(cholesky)/cholesky | solution.py:85
  646.2 0.7 compare_reduce_fusion.1
  646.9 0.6 compare_reduce_fusion
  647.5 0.7 compare_reduce_fusion.2
  650.7 0.1 select_bitcast_fusion
  650.9 0.0 copy-done
  650.9 1.3 copy.21
  (10 shorter events, 0.2 us)
Async XLA Ops:
  7.9 12.4 %collective-permute-start = (f32[16,512]{1,0:T(8,128)S(1)}, f32[16,512]{1,0:T(8,128)S(1)}, u32[]{:S(2)}, u32[]{:S(2)}) collective-permute-start(f32[16,512]{1,0:T(8,128)S(1)} %get-tuple-element.12), channel_id=1, source_target_pairs={{0,1},{1,2},{2,3},{3,4},{4,5},{5,6},{6,7},{7,8},{8,9},{9,10},{10,1... | collective-permute-start | bytes 98312 | tf_op jit(solution)/shard_map/ppermute | solution.py:12
  12.9 19.5 %collective-permute-start.1 = (f32[16,512]{1,0:T(8,128)S(1)}, f32[16,512]{1,0:T(8,128)S(1)}, u32[]{:S(2)}, u32[]{:S(2)}) collective-permute-start(f32[16,512]{1,0:T(8,128)S(1)} %get-tuple-element.13), channel_id=1, source_target_pairs={{1,0},{2,1},{3,2},{4,3},{5,4},{6,5},{7,6},{8,7},{9,8},{10,9},{11,1... | collective-permute-start | bytes 98312 | tf_op jit(solution)/shard_map/ppermute | solution.py:15
  209.3 188.4 %all-to-all-start = ((f32[32,128,512]{2,1,0:T(8,128)}), f32[32,128,512]{2,1,0:T(8,128)}, u32[]{:S(2)}, u32[]{:S(2)}) async-start(f32[32,128,512]{2,1,0:T(8,128)} %broadcast_select_fusion), calls=%async_computation | async-start | bytes 16777216 | tf_op jit(solution)/shard_map/all_to_all | solution.py:67
  216.3 347.8 %all-reduce.3.cloned.1.call-start = ((), (), s32[]{:S(2)}) async-start(), calls=%async_computation.1 | async-start | bytes 2097152 | tf_op jit(solution)/shard_map/psum | solution.py:84
  427.4 223.5 %copy-start = (f32[256,512]{1,0:T(8,128)}, f32[256,512]{1,0:T(8,128)S(1)}, u32[]{:S(2)}) copy-start(f32[256,512]{1,0:T(8,128)S(1)} %broadcast_select_fusion.1) | copy-start | bytes 1572868
Sparse Core Ops, SparseCore 0:
  429.5 134.5 all-reduce.2
where the time goes:
time: 664 us; the launch traced here: 659 us
  waiting for transfers between devices  315 us (47%)
  other arithmetic  212 us (32%)
  local copies, waits for them, and re-layouts  54.7 us (8%)
  matrix products  47 us (7%)
  between operations  17.3 us (3%)
  starting transfers between devices  13.3 us (2%)
    all_to_all x1, waiting for transfers between devices, on_device(): lax.all_to_all(outgoing, ('tm', 'grp'), split_axis=0, concat_axis=0, tile...  181 us
    psum x1, waiting for transfers between devices, on_device(): gram = lax.psum(local_gram, ('tm', 'grp'))  135 us
    mul x1, other arithmetic, on_device(): flipped = filtered * sign_flips.astype(jnp.float32)[:, None]  123 us
    another operation x14, other arithmetic, on_device(): lower = jnp.linalg.cholesky(gram / sample_count)  78.8 us
    gather x1, local copies, waits for them, and re-layouts, on_device(): outgoing = jnp.take(mixed, used_positions, axis=0)  21.4 us
    dot_general x1, matrix products, on_device(): jnp.einsum('op,pkw->okw', hadamard(devices_all), stacked, precision=lax.P...  16.9 us
    dot_general x1, matrix products, local_transform(): jnp.einsum('vy,uyw->uvw', hadamard(inner), layered, precision=lax.Precisi...  13.8 us
  transfers between devices with their start and end apart: 4, of which 2 were waited for; matrix products, arithmetic and copies ran while one was open for 3% of the time, Pallas kernels for 0%

commit v1 on v0

--- a/solution.py
+++ b/solution.py
@@ -1,7 +1,15 @@
+import functools
 import jax
 import jax.numpy as jnp
 from jax import lax
 from jax.sharding import PartitionSpec as P
+
+
+def _save_core(inner_x, which_axis):
+    return jnp.sum(lax.all_gather(inner_x, axis_name=which_axis), 0)
+
+
+try_all_the_series = functools.partial(_save_core, which_axis=("tm", "grp"))
 
 
 def extended(block, sides, width):
@@ -81,7 +89,7 @@
         precision=lax.Precision.HIGHEST,
         preferred_element_type=jnp.float32,
     )
-    gram = lax.psum(local_gram, ("tm", "grp"))
+    gram = try_all_the_series(local_gram)
     lower = jnp.linalg.cholesky(gram / sample_count)
     return (sketch, lower.T)
 

time: 664 us -> 743 us (1.12)
  waiting for transfers between devices: 315 us -> 379 us
  other arithmetic: 212 us -> 222 us
    all_gather x0 -> x1, waiting for transfers between devices: none -> 198 us  [_save_core(): return jnp.sum(lax.all_gather(inner_x, axis_name=which_axis), 0)]
    psum x1 -> x0, waiting for transfers between devices: 135 us -> none  [on_device(): gram = lax.psum(local_gram, ('tm', 'grp'))]
    reduce_sum x0 -> x1, other arithmetic: none -> 12.5 us  [_save_core(): return jnp.sum(lax.all_gather(inner_x, axis_name=which_axis), 0)]
where the time goes in v1:
time: 743 us; the launch traced here: 738 us
  waiting for transfers between devices  379 us (51%)
  other arithmetic  222 us (30%)
  local copies, waits for them, and re-layouts  55.7 us (7%)
  matrix products  50.8 us (7%)
  between operations  17.3 us (2%)
  starting transfers between devices  13.3 us (2%)
    all_gather x1, waiting for transfers between devices, _save_core(): return jnp.sum(lax.all_gather(inner_x, axis_name=which_axis), 0)  198 us
    all_to_all x1, waiting for transfers between devices, on_device(): lax.all_to_all(outgoing, ('tm', 'grp'), split_axis=0, concat_axis=0, tile...  181 us
    mul x1, other arithmetic, on_device(): flipped = filtered * sign_flips.astype(jnp.float32)[:, None]  123 us
    another operation x14, other arithmetic, on_device(): lower = jnp.linalg.cholesky(gram / sample_count)  78.7 us
    gather x1, local copies, waits for them, and re-layouts, on_device(): outgoing = jnp.take(mixed, used_positions, axis=0)  21.4 us
    dot_general x1, matrix products, on_device(): jnp.einsum('op,pkw->okw', hadamard(devices_all), stacked, precision=lax.P...  17.3 us
  transfers between devices with their start and end apart: 4, of which 2 were waited for; matrix products, arithmetic and copies ran while one was open for 3% of the time, Pallas kernels for 0%

profile of v1, /device:TPU:0, one launch (start us, length us, event | category | flops | bytes accessed | tf_op | source)
XLA Modules:
  0.0 737.6 jit_solution(364526677447432609)
XLA Ops:
  7.2 0.8 fusion.110
  7.9 4.9 collective-permute-start
  12.9 1.3 collective-permute-start.1
  14.2 1.4 slice.317
  15.6 2.1 fusion.111
  17.7 1.9 fusion.112
  19.6 0.7 convert_element_type.14
  20.3 0.0 collective-permute-done
  20.3 0.6 constant_dynamic-update-slice_fusion.1
  20.9 11.5 %constant_dynamic-update-slice_fusion = (f32[4112,512]{1,0:T(8,128)}, f32[4112,512]{1,0:T(8,128)}) fusion(f32[4112,512]{1,0:T(8,128)} %constant_dynamic-update-slice_fusion.1, f32[4096,512]{1,0:T(8,128)} %param.4), kind=kLoop, calls=%fused_computation.142 | loop fusion | bytes 25165824 | tf_op jit(solution)/shard_map/concatenate | solution.py:24
  32.4 0.0 collective-permute-done.1
  32.4 0.6 constant_dynamic-update-slice_fusion.2
  33.0 122.9 %fusion.1 = f32[4096,512]{1,0:T(8,128)S(1)} fusion(f32[4112,512]{1,0:T(8,128)} %constant_dynamic-update-slice_fusion.2, f32[4112,512]{1,0:T(8,128)} %get-tuple-element.10, f32[4096,512]{1,0:T(8,128)} %param.4, f32[4096]{0:T(1024)S(1)} %convert_element_type.14, f32[]{:T(128)} %bitcast.35, f32[]{:T(128)} %bitcast.34, f32[]{:T(128)} %bitcast.33, f32[]{:T(128)} %bitcast.32, ...), kind=kLoop, calls=%fused_computation.4 | loop fusion | flops 138412032 | bytes 285229184 | tf_op jit(solution)/shard_map/mul | solution.py:65
  156.0 12.4 %fusion.37 = f32[64,64,512]{2,0,1:T(8,128)S(1)} fusion(f32[64,64,512]{2,1,0:T(8,128)S(1)} %bitcast.78), kind=kOutput, calls=%fused_computation.71 | convolution fusion | flops 1610715136 | bytes 16777216 | tf_op jit(solution)/shard_map/ux,xvw->uvw/dot_general | solution.py:48
  168.4 13.6 %fusion.35 = f32[64,512,64]{1,2,0:T(8,128)} fusion(f32[64,64,512]{2,0,1:T(8,128)S(1)} %fusion.37), kind=kOutput, calls=%fused_computation.69 | convolution fusion | flops 1610715136 | bytes 16777216 | tf_op jit(solution)/shard_map/vy,uyw->uvw/dot_general | solution.py:49
  182.0 21.4 %gather_fusion = f32[4096,512]{1,0:T(8,128)} fusion(f32[4096,512]{1,0:T(8,128)} %bitcast.76, s32[4096]{0:T(1024)S(1)} %broadcast_clamp_fusion), kind=kCustom, calls=%fused_computation | custom fusion | bytes 16793600 | tf_op jit(solution)/shard_map/jit(_take)/gather | solution.py:74
  203.4 5.8 broadcast_select_fusion
  209.3 7.0 all-to-all-start
  216.3 0.0 all-gather.3.cloned.1.call-start
  216.3 0.8 compare_and_fusion
  217.1 180.5 %all-to-all-done = f32[32,128,512]{2,1,0:T(8,128)} async-done(((f32[32,128,512]{2,1,0:T(8,128)}), f32[32,128,512]{2,1,0:T(8,128)}, u32[]{:S(2)}, u32[]{:S(2)}) %all-to-all-start) | async-done | bytes 8388640 | tf_op jit(solution)/shard_map/all_to_all | solution.py:75
  397.7 17.3 %broadcast_multiply_fusion = f32[32,128,512]{2,0,1:T(8,128)S(1)} fusion(f32[32,128,512]{2,1,0:T(8,128)} %all-to-all-done), kind=kOutput, calls=%fused_computation.73 | convolution fusion | flops 807426048 | bytes 16777216 | tf_op jit(solution)/shard_map/op,pkw->okw/dot_general | solution.py:78
  415.0 8.1 %copy.16 = f32[32,128,512]{2,1,0:T(8,128)} copy(f32[32,128,512]{2,0,1:T(8,128)S(1)} %broadcast_multiply_fusion) | data formatting | bytes 16777216 | tf_op jit(solution)/shard_map/mul | solution.py:78
  423.1 4.6 gather_fusion.1
  427.7 0.1 broadcast_select_fusion.1
  427.8 0.0 copy-start
  427.8 2.0 fusion.113
  429.8 0.0 all-gather.3.cloned.1.call-update
  429.8 198.1 %all-gather.3.cloned.1.call-done = f32[16384,512]{1,0:T(8,128)} async-done(((f32[512,512]{1,0:T(8,128)}), f32[16384,512]{1,0:T(8,128)}) %all-gather.3.cloned.1.call-update) | async-done | bytes 33554448 | tf_op jit(solution)/shard_map/all_gather | solution.py:9
  627.9 12.5 %reduce_sum.11 = f32[512,512]{1,0:T(8,128)S(1)} reduce(f32[32,512,512]{2,1,0:T(8,128)} %bitcast.79, f32[]{:T(128)} %constant.234.clone.1), dimensions={0}, to_apply=%region_0.1 | reduce | flops 8126464 | bytes 34603012 | tf_op jit(solution)/shard_map/reduce_sum | solution.py:9
  640.4 0.0 copy-done
  640.4 0.3 copy.17
  640.8 0.2 fusion.41
  641.0 0.0 copy-start.1
  641.0 1.0 copy-done.1
  642.0 11.7 %cholesky.104 = f32[128,128]{1,0:T(8,128)S(1)} custom-call(f32[128,128]{1,0:T(8,128)S(1)} %cholesky.266), custom_call_target="Cholesky" | custom-call | tf_op jit(solution)/shard_map/jit(cholesky)/cholesky | solution.py:93
  653.7 0.1 cholesky.224
  653.9 9.8 %custom-call.27 = f32[1,128,128]{1,2,0:T(8,128)S(1)} custom-call(f32[1,128,128]{2,1,0:T(8,128)S(1)} %get-tuple-element.23), custom_call_target="InvertDiagBlocksLowerTriangular" | custom-call | tf_op jit(solution)/shard_map/jit(cholesky)/cholesky | solution.py:93
  663.7 1.2 constant_dynamic-update-slice_fusion.6
  664.9 1.3 convolution_subtract_fusion
  666.2 11.7 %cholesky.217 = f32[128,128]{1,0:T(8,128)S(1)} custom-call(f32[128,128]{1,0:T(8,128)S(1)} %cholesky.270), custom_call_target="Cholesky" | custom-call | tf_op jit(solution)/shard_map/jit(cholesky)/cholesky | solution.py:93
  677.9 10.0 %custom-call.28 = f32[1,128,128]{1,2,0:T(8,128)S(1)} custom-call(f32[1,128,128]{2,1,0:T(8,128)S(1)} %get-tuple-element.20), custom_call_target="InvertDiagBlocksLowerTriangular" | custom-call | tf_op jit(solution)/shard_map/jit(cholesky)/cholesky | solution.py:93
  688.0 0.3 convolution_dynamic-update-slice_fusion
  688.3 1.3 convolution_subtract_fusion.1
  689.6 11.7 %cholesky.238 = f32[128,128]{1,0:T(8,128)S(1)} custom-call(f32[128,128]{1,0:T(8,128)S(1)} %cholesky.275), custom_call_target="Cholesky" | custom-call | tf_op jit(solution)/shard_map/jit(cholesky)/cholesky | solution.py:93
  701.3 0.7 compare_reduce_fusion.1
  702.0 9.8 %custom-call.29 = f32[1,128,128]{1,2,0:T(8,128)S(1)} custom-call(f32[1,128,128]{2,1,0:T(8,128)S(1)} %get-tuple-element.17), custom_call_target="InvertDiagBlocksLowerTriangular" | custom-call | tf_op jit(solution)/shard_map/jit(cholesky)/cholesky | solution.py:93
  711.8 0.2 convolution_dynamic-update-slice_fusion.1
  712.1 1.2 convolution_subtract_fusion.2
  713.3 11.7 %cholesky.255 = f32[128,128]{1,0:T(8,128)S(1)} custom-call(f32[128,128]{1,0:T(8,128)S(1)} %convolution_subtract_fusion.2), custom_call_target="Cholesky" | custom-call | tf_op jit(solution)/shard_map/jit(cholesky)/cholesky | solution.py:93
  725.0 0.6 compare_reduce_fusion
  725.7 0.7 compare_reduce_fusion.2
  728.9 0.1 select_bitcast_fusion
  729.0 1.3 copy.18
  (10 shorter events, 0.2 us)
Async XLA Ops:
  7.9 12.4 %collective-permute-start = (f32[16,512]{1,0:T(8,128)S(1)}, f32[16,512]{1,0:T(8,128)S(1)}, u32[]{:S(2)}, u32[]{:S(2)}) collective-permute-start(f32[16,512]{1,0:T(8,128)S(1)} %get-tuple-element.12), channel_id=1, source_target_pairs={{0,1},{1,2},{2,3},{3,4},{4,5},{5,6},{6,7},{7,8},{8,9},{9,10},{10,1... | collective-permute-start | bytes 98312 | tf_op jit(solution)/shard_map/ppermute | solution.py:20
  12.9 19.5 %collective-permute-start.1 = (f32[16,512]{1,0:T(8,128)S(1)}, f32[16,512]{1,0:T(8,128)S(1)}, u32[]{:S(2)}, u32[]{:S(2)}) collective-permute-start(f32[16,512]{1,0:T(8,128)S(1)} %get-tuple-element.13), channel_id=1, source_target_pairs={{1,0},{2,1},{3,2},{4,3},{5,4},{6,5},{7,6},{8,7},{9,8},{10,9},{11,1... | collective-permute-start | bytes 98312 | tf_op jit(solution)/shard_map/ppermute | solution.py:23
  209.3 188.4 %all-to-all-start = ((f32[32,128,512]{2,1,0:T(8,128)}), f32[32,128,512]{2,1,0:T(8,128)}, u32[]{:S(2)}, u32[]{:S(2)}) async-start(f32[32,128,512]{2,1,0:T(8,128)} %broadcast_select_fusion), calls=%async_computation | async-start | bytes 16777216 | tf_op jit(solution)/shard_map/all_to_all | solution.py:75
  216.3 411.6 %all-gather.3.cloned.1.call-start = ((), (), s32[]{:S(2)}) async-start(), calls=%async_computation.1 | async-start | bytes 34603008 | tf_op jit(solution)/shard_map/all_gather | solution.py:9
  427.8 212.7 %copy-start = (f32[256,512]{1,0:T(8,128)}, f32[256,512]{1,0:T(8,128)S(1)}, u32[]{:S(2)}) copy-start(f32[256,512]{1,0:T(8,128)S(1)} %broadcast_select_fusion.1) | copy-start | bytes 1572868
  641.0 1.0 copy-start.1
Sparse Core Ops, SparseCore 0:
  429.9 197.9 all-gather.2
